TPU v7x, 512 devices: a whole 4x4x16 slice. The times are simulated.
512 devices in a mesh: req: 64 (over z, y), tensor: 8 (over x, core).
Axes of the slice: x: 4, y: 4, z: 16, core: 2. Of those that a mesh axis runs over, the one named last changes fastest.
Arguments:
- tokens: bfloat16 [16384, 2048], P('req', 'tensor'), may hold values from -6 to 6
- segment_ids: int32 [16384], P('req'), may hold values from 0 to 42, as said below
- prefix_lengths: int32 [43], replicated, may hold values from 0 to 256, as said below
- page_owner: int32 [4096, 1], P('req'), may hold values from 0 to 63; in each aligned block of 64 rows (0 to 63, 64 to 127, ...) at most 2 rows name the same one
- slot_perm: int32 [64, 128], P('req'), may hold values from 0 to 127, each once within a row
- ln_gain: float32 [2048], replicated, may hold values from 0.1 to 1.9
- ln_bias: float32 [2048], replicated, may hold values from -3 to 3
- qkv_weight: bfloat16 [2048, 3, 2048], P('req', None, 'tensor')
- qkv_bias: float32 [3, 2048], P(None, 'tensor'), may hold values from -3 to 3
- dense_weight: bfloat16 [2048, 2048], P('tensor', 'req'), may hold values from -0.375 to 0.375
- dense_bias: float32 [2048], P('tensor'), may hold values from -3 to 3
- fc1_weight: bfloat16 [2048, 4096], P('req', 'tensor'), may hold values from -0.125 to 0.125
- fc1_bias: float32 [4096], P('tensor'), may hold values from -3 to 3
- fc2_weight: bfloat16 [4096, 2048], P('tensor', 'req'), may hold values from -0.25 to 0.25
- fc2_bias: float32 [2048], P('tensor'), may hold values from -3 to 3
- prefix_cache: bfloat16 [16384, 2, 2048], P('req', None, 'tensor'), may hold values from -9 to 9
- cache_pool: bfloat16 [32768, 2, 2048], P('req', None, 'tensor'), may hold values from -6 to 6
Outputs:
- layer_out: bfloat16 [16384, 2048], P('req', 'tensor')
- new_pool: bfloat16 [32768, 2, 2048], P('req', None, 'tensor')
Inputs may be any that keep to these rules, and one draw needn't show every extreme that they name: `segment_ids`: labels 1 to 42 appear in order, each as one run of 257 to 512 rows, together filling all rows before the padding; segment 1 is 512 rows long; the last 128 rows are 0. `prefix_lengths`: entry 0 is 0 and entry 1 is 256. `page_owner`: among the pages of one index of req no owner appears more than 2 times, and some owner appears exactly 2 times. `slot_perm`: each row is a permutation of 0 to 127.
All inputs are finite; a program needn't handle non-finite values.
Results may differ from a plain program's by a relative error of at most 0.006.
The roundings to bfloat16 on the way count: a program that leaves them out, or rounds other values in their place, can miss the bound.
Values may be sent and summed in bfloat16 or wider, within the bound.
A program may use at most 64 MiB of HBM per device.

v0:
```python
import jax
import jax.numpy as jnp
from jax import lax
from jax.sharding import PartitionSpec as P

HEAD_DIM = 64
ROT = 32
SPAN = 2
SINKS = 4
PAGE = 4
WINDOW = 512
EPSILON = 1e-05


def from_behind(value, axis, steps):
    count = lax.axis_size(axis)
    leading, last = (max(0, -steps), min(count, count - steps))
    return lax.ppermute(value, axis, [(source, source + steps) for source in range(leading, last)])


def norm_rows(widened, gain, offset_bias):
    average = jnp.mean(widened, axis=-1, keepdims=True)
    centred = widened - average
    spread = jnp.mean(centred * centred, axis=-1, keepdims=True)
    return (centred * lax.rsqrt(spread + EPSILON) * gain + offset_bias).astype(jnp.bfloat16)


def label_rows(places, starts, prefix_lengths):
    labels = jnp.arange(starts.shape[0], dtype=jnp.int32)
    passed = (starts[None, :] <= places[:, None]) & (labels[None, :] >= 1)
    counted = jnp.sum(passed.astype(jnp.int32), axis=1)
    segment = jnp.where(places >= starts[0], 0, counted)
    segment = jnp.where(places < 0, -2, segment)
    onehot = segment[:, None] == labels[None, :]
    earliest = jnp.sum(jnp.where(onehot, starts[None, :], 0), axis=1)
    offset = jnp.sum(jnp.where(onehot, prefix_lengths[None, :], 0), axis=1)
    return (segment, offset + places - earliest)


def prefix_rows(block_id, rows_dev, prefix_count, starts, prefix_lengths):
    labels = jnp.arange(starts.shape[0], dtype=jnp.int32)
    located = (starts >= block_id * rows_dev) & (starts < (block_id + 1) * rows_dev) & (labels >= 1)
    owner_label = jnp.sum(jnp.where(located, labels, 0))
    length = jnp.sum(jnp.where(located, prefix_lengths, 0))
    places = jnp.arange(prefix_count, dtype=jnp.int32)
    usable = jnp.any(located) & (places < length)
    return (jnp.where(usable, owner_label, -2), places)


def rotate_heads(values, position):
    half_rot = ROT // 2
    frequency = 10000.0 ** (-2.0 * jnp.arange(half_rot, dtype=jnp.float32) / ROT)
    angles = position.astype(jnp.float32)[:, None] * frequency[None, :]
    cosine = jnp.cos(angles)[:, None, :]
    sine_vals = jnp.sin(angles)[:, None, :]
    lower = values[..., :half_rot]
    upper = values[..., half_rot:ROT]
    return jnp.concatenate(
        [lower * cosine - upper * sine_vals, upper * cosine + lower * sine_vals, values[..., ROT:]],
        axis=-1,
    )


def head_attention(query_rows, key_rows, value_rows, allowed):
    head_count = query_rows.shape[1] // HEAD_DIM
    score_scale = HEAD_DIM ** (-0.5)

    def one_head(head_index):
        query_cols = lax.dynamic_slice_in_dim(query_rows, head_index * HEAD_DIM, HEAD_DIM, 1)
        key_cols = lax.dynamic_slice_in_dim(key_rows, head_index * HEAD_DIM, HEAD_DIM, 1)
        value_cols = lax.dynamic_slice_in_dim(value_rows, head_index * HEAD_DIM, HEAD_DIM, 1)
        scores = (
            lax.dot_general(
                query_cols, key_cols, (((1,), (1,)), ((), ())), preferred_element_type=jnp.float32
            )
            * score_scale
        )
        masked = jnp.where(allowed, scores, -1e30)
        highest = jnp.max(masked, axis=1, keepdims=True)
        expo = jnp.where(allowed, jnp.exp(masked - highest), 0.0)
        denom = jnp.sum(expo, axis=1, keepdims=True)
        mixed = (
            jnp.dot(expo.astype(jnp.bfloat16), value_cols, preferred_element_type=jnp.float32)
            / denom
        )
        return mixed.astype(jnp.bfloat16)

    outcome = lax.map(one_head, jnp.arange(head_count, dtype=jnp.int32))
    return jnp.transpose(outcome, (1, 0, 2)).reshape(query_rows.shape[0], head_count * HEAD_DIM)


def shards(
    tokens,
    segment_ids,
    prefix_lengths,
    page_owner,
    slot_perm,
    ln_gain,
    ln_bias,
    qkv_weight,
    qkv_bias,
    dense_weight,
    dense_bias,
    fc1_weight,
    fc1_bias,
    fc2_weight,
    fc2_bias,
    prefix_cache,
    cache_pool,
):
    req_count = lax.axis_size("req")
    req_index = lax.axis_index("req")
    tok_rows = tokens.shape[0]
    prefix_count = prefix_cache.shape[0]
    head_cols = qkv_weight.shape[2]
    pool_count = slot_perm.shape[1]
    page_cap = pool_count // req_count
    gathered = lax.all_gather(tokens, "tensor", axis=1, tiled=True)
    normed = norm_rows(gathered.astype(jnp.float32), ln_gain, ln_bias)
    row_ids = jnp.arange(tok_rows, dtype=jnp.int32)
    places = req_index * tok_rows + row_ids
    labels = jnp.arange(prefix_lengths.shape[0], dtype=jnp.int32)
    beyond = tok_rows * req_count
    earliest_rows = jnp.min(
        jnp.where(segment_ids[:, None] == labels[None, :], places[:, None], beyond), axis=0
    )
    starts = lax.pmin(earliest_rows, "req")

    def add_rows(portion):
        return jnp.dot(normed, portion, preferred_element_type=jnp.float32)

    qkv_local = qkv_weight.reshape(qkv_weight.shape[0], 3 * head_cols)
    projected = add_rows(lax.all_gather(qkv_local, "req", axis=0, tiled=True))
    lifted = add_rows(lax.all_gather(fc1_weight, "req", axis=0, tiled=True))
    projected = (projected + qkv_bias.reshape(1, 3 * head_cols)).reshape(
        tok_rows, 3, head_cols // HEAD_DIM, HEAD_DIM
    )
    segment, position = label_rows(places, starts, prefix_lengths)
    queries = (
        rotate_heads(projected[:, 0], position).astype(jnp.bfloat16).reshape(tok_rows, head_cols)
    )
    new_keys = (
        rotate_heads(projected[:, 1], position).astype(jnp.bfloat16).reshape(tok_rows, head_cols)
    )
    new_values = projected[:, 2].astype(jnp.bfloat16).reshape(tok_rows, head_cols)
    key_value = jnp.stack([new_keys, new_values], axis=1)
    pages_here = tok_rows // PAGE
    pages = key_value.reshape(pages_here, PAGE * 2 * head_cols)
    owners = page_owner[:, 0]
    onehot = (owners[:, None] == jnp.arange(req_count, dtype=jnp.int32)[None, :]).astype(jnp.int32)
    earlier = jnp.cumsum(onehot, axis=0) - onehot
    earlier_count = jnp.sum(earlier * onehot, axis=1)
    target = owners * page_cap + earlier_count
    selecting = (target[None, :] == jnp.arange(pool_count, dtype=jnp.int32)[:, None]).astype(
        jnp.bfloat16
    )
    outgoing = jnp.dot(selecting, pages, preferred_element_type=jnp.float32).astype(jnp.bfloat16)
    filled = jnp.sum(selecting, axis=1)
    incoming, incoming_filled = (
        lax.all_to_all(
            outgoing.reshape(req_count, page_cap, PAGE * 2 * head_cols),
            "req",
            split_axis=0,
            concat_axis=0,
            tiled=True,
        ),
        lax.all_to_all(
            filled.reshape(req_count, page_cap), "req", split_axis=0, concat_axis=0, tiled=True
        ),
    )
    slot_ids = slot_perm[0]
    placing = (slot_ids[None, :] == jnp.arange(pool_count, dtype=jnp.int32)[:, None]) & (
        incoming_filled.reshape(pool_count)[None, :] > 0
    )
    written = jnp.dot(
        placing.astype(jnp.bfloat16),
        incoming.reshape(pool_count, PAGE * 2 * head_cols),
        preferred_element_type=jnp.float32,
    ).astype(jnp.bfloat16)
    written_mask = jnp.any(placing, axis=1)
    pool_pages = cache_pool.reshape(pool_count, PAGE * 2 * head_cols)
    new_pool = jnp.where(written_mask[:, None], written, pool_pages).reshape(cache_pool.shape)
    local_keys = jnp.concatenate([key_value, prefix_cache], axis=0)
    blocks = [local_keys]
    for shift_by in range(1, SPAN + 1):
        blocks.append(from_behind(local_keys, "req", shift_by))
    key_segs = []
    key_poss = []
    for step_back in range(SPAN + 1):
        block_id = req_index - step_back
        seg_new, pos_new = label_rows(block_id * tok_rows + row_ids, starts, prefix_lengths)
        seg_old, pos_old = prefix_rows(block_id, tok_rows, prefix_count, starts, prefix_lengths)
        key_segs.extend([seg_new, seg_old])
        key_poss.extend([pos_new, pos_old])
    key_segment = jnp.concatenate(key_segs)
    key_position = jnp.concatenate(key_poss)
    allowed = (key_segment[None, :] == segment[:, None]) & (
        key_position[None, :] <= position[:, None]
    )
    allowed = allowed & (
        (position[:, None] - key_position[None, :] < WINDOW) | (key_position[None, :] < SINKS)
    )
    all_keys = jnp.concatenate(blocks, axis=0)
    attended = head_attention(queries, all_keys[:, 0, :], all_keys[:, 1, :], allowed)
    hidden = jax.nn.gelu(lifted + fc1_bias, approximate=True).astype(jnp.bfloat16)
    attn_part = jnp.dot(
        attended,
        lax.all_gather(dense_weight, "req", axis=1, tiled=True),
        preferred_element_type=jnp.float32,
    )
    mlp_part = jnp.dot(
        hidden,
        lax.all_gather(fc2_weight, "req", axis=1, tiled=True),
        preferred_element_type=jnp.float32,
    )
    branches = attn_part + mlp_part
    summed = lax.psum_scatter(branches, "tensor", scatter_dimension=1, tiled=True)
    layer_out = (tokens.astype(jnp.float32) + summed + dense_bias + fc2_bias).astype(jnp.bfloat16)
    return (layer_out, new_pool)


def solution(mesh):
    placed = (
        P("req", "tensor"),
        P("req"),
        P(),
        P("req", None),
        P("req", None),
        P(),
        P(),
        P("req", None, "tensor"),
        P(None, "tensor"),
        P("tensor", "req"),
        P("tensor"),
        P("req", "tensor"),
        P("tensor"),
        P("tensor", "req"),
        P("tensor"),
        P("req", None, "tensor"),
        P("req", None, "tensor"),
    )
    return jax.shard_map(
        shards,
        mesh=mesh,
        in_specs=placed,
        out_specs=(P("req", "tensor"), P("req", None, "tensor")),
        check_vma=False,
    )
```

profile of v0, /device:TPU:2, one launch (start us, length us, event | category | flops | bytes accessed | tf_op | source)
XLA Modules:
  0.0 680.2 jit_solution(15321426984740319894)
XLA Ops:
  7.2 0.7 all-gather.6.cloned.1.call-update
  8.0 1.4 copy.51
  9.5 0.7 all-gather.10.cloned.1.call-update
  10.2 0.5 all-gather.12.cloned.1.call-update
  10.8 0.5 all-gather.14.cloned.1.call-update
  11.4 0.8 select_reduce_fusion.6
  12.2 34.2 %pmin.7 = s32[43]{0:T(128)S(1)} all-reduce(s32[43]{0:T(128)S(1)} %select_reduce_fusion.6), channel_id=1, replica_groups=mesh['req'=64,'tensor'=8] {'req'}, use_global_device_ids=true, to_apply=%region_3.4 | all-reduce | flops 43 | bytes 344 | tf_op jit(solution)/shard_map/pmin | solution.py:127
  46.4 0.7 fusion.57
  47.1 1.4 select_reduce_fusion.9
  48.5 0.7 reduce_or.36
  49.4 1.9 constant_dynamic-update-slice_fusion.8
  51.3 1.9 constant_dynamic-update-slice_fusion.4
  53.3 0.8 select_reduce_fusion.5
  54.1 0.7 add.182
  54.8 1.1 copy.42
  56.2 1.5 convert_reduce_fusion
  57.7 1.6 fusion.23
  59.4 134.8 %all-gather.8.cloned.1.call-done = bf16[2048,768]{1,0:T(8,128)(2,1)} async-done(((bf16[32,768]{1,0:T(8,128)(2,1)}), bf16[2048,768]{1,0:T(8,128)(2,1)}) %all-gather.8.cloned.1.call-update) | async-done | bytes 3145744 | tf_op jit(solution)/shard_map/all_gather | solution.py:133
  194.2 3.0 convolution_add_fusion.1
  197.2 0.3 copy.40
  197.7 1.9 collective-permute-start
  199.6 4.1 collective-permute-start.1
  203.7 1.9 constant_dynamic-update-slice_fusion
  205.7 2.8 collective-permute-done
  208.5 5.8 collective-permute-done.1
  214.5 15.9 %while.11 = (s32[]{:T(128)}, bf16[4,256,64]{1,2,0:T(8,128)(2,1)S(1)}, s32[4]{0:T(128)S(1)}, bf16[256,256]{0,1:T(8,128)(2,1)S(1)}, bf16[1536,256]{0,1:T(8,128)(2,...) while((s32[]{:T(128)}, ...), condition=%wide.region_25.26_spmd.clone, body=%wide.region_22.25_spmd.clone.sunk | while | flops 112492032 | bytes 5240527 | solution.py:88
  214.5 0.6 dynamic_slice.34
  215.8 0.9 fusion.74
  216.7 0.9 fusion.75
  217.6 0.9 fusion.76
  218.5 0.6 dynamic_slice.34
  219.8 0.9 fusion.74
  220.6 0.9 fusion.75
  221.6 0.9 fusion.76
  222.5 0.6 dynamic_slice.34
  223.7 0.9 fusion.74
  224.6 0.9 fusion.75
  225.5 0.9 fusion.76
  226.5 0.6 dynamic_slice.34
  227.7 0.9 fusion.74
  228.6 0.9 fusion.75
  229.5 0.9 fusion.76
  230.4 100.3 %all-gather.10.cloned.1.call-done = bf16[256,2048]{0,1:T(8,128)(2,1)} async-done(((bf16[256,32]{0,1:T(8,128)(2,1)}), bf16[256,2048]{0,1:T(8,128)(2,1)}) %all-gather.10.cloned.1.call-update) | async-done | bytes 1048592 | tf_op jit(solution)/shard_map/all_gather | solution.py:208
  330.7 1.7 fusion.59
  332.5 138.2 %all-gather.12.cloned.1.call-done = bf16[2048,512]{1,0:T(8,128)(2,1)} async-done(((bf16[32,512]{1,0:T(8,128)(2,1)}), bf16[2048,512]{1,0:T(8,128)(2,1)}) %all-gather.12.cloned.1.call-update) | async-done | bytes 2097168 | tf_op jit(solution)/shard_map/all_gather | solution.py:134
  470.7 139.8 %all-gather.14.cloned.1.call-done = bf16[512,2048]{0,1:T(8,128)(2,1)} async-done(((bf16[512,32]{0,1:T(8,128)(2,1)}), bf16[512,2048]{0,1:T(8,128)(2,1)}) %all-gather.14.cloned.1.call-update) | async-done | bytes 2097168 | tf_op jit(solution)/shard_map/all_gather | solution.py:213
  610.5 5.1 convolution_add_fusion
  615.6 0.6 copy-done.3
  616.4 0.2 select_reduce_fusion.7
  616.7 0.8 all_to_all.12
  617.5 10.3 %all-to-all-start = ((bf16[64,1,2]{2,1,0:T(2,128)(2,1)}), bf16[64,1,2]{2,1,0:T(2,128)(2,1)S(1)}, u32[]{:S(2)}, u32[]{:S(2)}) async-start(bf16[64,1,2]{2,1,0:T(2,128)(2,1)} %all_to_all.12), calls=%async_computation.1 | async-start | bytes 65536 | tf_op jit(solution)/shard_map/all_to_all | solution.py:167
  627.8 0.2 copy.47
  628.0 0.2 reshape.253
  628.2 0.4 convolution_convert_fusion.1
  628.6 1.1 reshape.254
  629.7 12.6 %all-to-all-done = bf16[64,1,2]{2,1,0:T(2,128)(2,1)S(1)} async-done(((bf16[64,1,2]{2,1,0:T(2,128)(2,1)}), bf16[64,1,2]{2,1,0:T(2,128)(2,1)S(1)}, u32[]{:S(2)}, u32[]{:S(2)}) %all-to-all-start) | async-done | bytes 288 | tf_op jit(solution)/shard_map/all_to_all | solution.py:167
  642.4 4.6 all-to-all-start.1
  647.0 0.4 reshape.256
  647.6 0.1 gt.16
  647.8 22.2 %all-to-all-done.1 = bf16[64,2,2048]{2,1,0:T(2,128)(2,1)S(1)} async-done(((bf16[64,2,2048]{2,1,0:T(2,128)(2,1)}), bf16[64,2,2048]{2,1,0:T(2,128)(2,1)S(1)}, u32[]{:S(2)}, u32[]{:S(2)}) %all-to-all-start.1) | async-done | bytes 524320 | tf_op jit(solution)/shard_map/all_to_all | solution.py:160
  670.0 0.2 reshape.255
  670.2 0.3 fusion.22
  670.5 1.2 reshape.257
  671.7 1.7 add_convert_fusion
  (69 shorter events, 1.7 us)
Async XLA Ops:
  7.2 187.0 %copy-start.9 = (f32[2048]{0:T(1024)S(1)}, f32[2048]{0:T(1024)}, u32[]{:S(2)}) copy-start(f32[2048]{0:T(1024)} %param.24) | copy-start | bytes 24580
  7.2 187.0 %copy-start.7 = (f32[2048]{0:T(1024)S(1)}, f32[2048]{0:T(1024)}, u32[]{:S(2)}) copy-start(f32[2048]{0:T(1024)} %param.25) | copy-start | bytes 24580
  7.2 49.0 %all-gather.6.cloned.1.call-start = ((), (), s32[]{:S(2)}) async-start(), calls=%async_computation.3 | async-start | bytes 1179648 | tf_op jit(solution)/shard_map/all_gather | solution.py:118
  7.9 186.3 %all-gather.8.cloned.1.call-start = ((), (), s32[]{:S(2)}) async-start(), calls=%async_computation.4 | async-start | bytes 3194880 | tf_op jit(solution)/shard_map/all_gather | solution.py:133
  9.4 321.3 %all-gather.10.cloned.1.call-start = ((), (), s32[]{:S(2)}) async-start(), calls=%async_computation.5 | async-start | bytes 1064960 | tf_op jit(solution)/shard_map/all_gather | solution.py:208
  10.2 460.5 %all-gather.12.cloned.1.call-start = ((), (), s32[]{:S(2)}) async-start(), calls=%async_computation.6 | async-start | bytes 2129920 | tf_op jit(solution)/shard_map/all_gather | solution.py:134
  10.7 599.7 %all-gather.14.cloned.1.call-start = ((), (), s32[]{:S(2)}) async-start(), calls=%async_computation.7 | async-start | bytes 2129920 | tf_op jit(solution)/shard_map/all_gather | solution.py:213
  11.3 660.4 %reduce-scatter.2.cloned.1.call-start = ((), (), s32[]{:S(2)}) async-start(), calls=%async_computation.8 | async-start | bytes 2359296 | tf_op jit(solution)/shard_map/reduce_scatter | solution.py:217
  56.1 138.1 %copy-start = (bf16[256,2048]{1,0:T(8,128)(2,1)S(1)}, bf16[256,2048]{1,0:T(8,128)(2,1)}, u32[]{:S(2)}) copy-start(bf16[256,2048]{1,0:T(8,128)(2,1)} %all-gather.6.cloned.1.call-done) | copy-start | bytes 3145732
  197.7 10.8 %collective-permute-start = (bf16[512,2,256]{0,2,1:T(8,128)(2,1)S(1)}, bf16[512,2,256]{0,2,1:T(8,128)(2,1)S(1)}, u32[]{:S(2)}, u32[]{:S(2)}) collective-permute-start(bf16[512,2,256]{0,2,1:T(8,128)(2,1)S(1)} %pad_maximum_fusion.1), channel_id=1, source_target_pairs={{0,8},{8,16},{16,24},{24,32},{32,40},{40,48},{48,56},{56,64},{64,7... | collective-permute-start | bytes 1572872 | tf_op jit(solution)/shard_map/ppermute | solution.py:18
  199.6 14.6 %collective-permute-start.1 = (bf16[512,2,256]{0,2,1:T(8,128)(2,1)S(1)}, bf16[512,2,256]{0,2,1:T(8,128)(2,1)S(1)}, u32[]{:S(2)}, u32[]{:S(2)}) collective-permute-start(bf16[512,2,256]{0,2,1:T(8,128)(2,1)S(1)} %pad_maximum_fusion.1), channel_id=1, source_target_pairs={{0,16},{8,24},{16,32},{24,40},{32,48},{40,56},{48,64},{56,72},{64,... | collective-permute-start | bytes 1572872 | tf_op jit(solution)/shard_map/ppermute | solution.py:18
  230.4 380.0 %copy-start.8 = (f32[2048]{0:T(1024)S(1)}, f32[2048]{0:T(1024)}, u32[]{:S(2)}) copy-start(f32[2048]{0:T(1024)} %param.25) | copy-start | bytes 24580
  615.6 0.7 copy-start.3
  617.5 24.9 %all-to-all-start = ((bf16[64,1,2]{2,1,0:T(2,128)(2,1)}), bf16[64,1,2]{2,1,0:T(2,128)(2,1)S(1)}, u32[]{:S(2)}, u32[]{:S(2)}) async-start(bf16[64,1,2]{2,1,0:T(2,128)(2,1)} %all_to_all.12), calls=%async_computation.1 | async-start | bytes 65536 | tf_op jit(solution)/shard_map/all_to_all | solution.py:167
  627.8 19.2 %copy-start.1 = (bf16[512,2,256]{2,1,0:T(2,128)(2,1)S(1)}, bf16[512,2,256]{2,1,0:T(2,128)(2,1)}, u32[]{:S(2)}) copy-start(bf16[512,2,256]{2,1,0:T(2,128)(2,1)} %param.35) | copy-start | bytes 1572868
  628.2 19.5 %copy-start.6 = (s32[1,128]{1,0:T(1,128)S(1)}, s32[1,128]{1,0:T(1,128)}, u32[]{:S(2)}) copy-start(s32[1,128]{1,0:T(1,128)} %param.23) | copy-start | bytes 1540
  642.4 27.6 %all-to-all-start.1 = ((bf16[64,2,2048]{2,1,0:T(2,128)(2,1)}), bf16[64,2,2048]{2,1,0:T(2,128)(2,1)S(1)}, u32[]{:S(2)}, u32[]{:S(2)}) async-start(bf16[64,2,2048]{2,1,0:T(2,128)(2,1)} %reshape.254), calls=%async_computation.2 | async-start | bytes 1048576 | tf_op jit(solution)/shard_map/all_to_all | solution.py:160
  647.4 24.3 %copy-start.2 = (bf16[256,256]{1,0:T(8,128)(2,1)S(1)}, bf16[256,256]{1,0:T(8,128)(2,1)}, u32[]{:S(2)}) copy-start(bf16[256,256]{1,0:T(8,128)(2,1)} %param.19) | copy-start | bytes 393220
  647.4 24.3 %copy-start.4 = (f32[256]{0:T(256)S(1)}, f32[256]{0:T(256)}, u32[]{:S(2)}) copy-start(f32[256]{0:T(256)} %param.33) | copy-start | bytes 3076
  647.4 24.3 %copy-start.5 = (f32[256]{0:T(256)S(1)}, f32[256]{0:T(256)}, u32[]{:S(2)}) copy-start(f32[256]{0:T(256)} %param.29) | copy-start | bytes 3076
Sparse Core Ops, SparseCore 0:
  10.1 34.8 all-gather.5
  48.6 145.5 all-gather.7
  197.1 133.5 all-gather.9
  333.5 137.0 all-gather.11
  473.5 136.9 all-gather.13
  615.7 34.3 reduce-scatter.1
where the time goes:
time: 681 us; the launch traced here: 680 us
  waiting for transfers between devices  559 us (82%)
  blocking collectives  34.2 us (5%)
  starting transfers between devices  21.1 us (3%)
  other arithmetic  20 us (3%)
  matrix products  17.7 us (3%)
  between operations  14.6 us (2%)
  local copies, waits for them, and re-layouts  10.9 us (2%)
    all_gather x1, waiting for transfers between devices, shards(): lax.all_gather(fc2_weight, 'req', axis=1, tiled=True)  140 us
    all_gather x1, waiting for transfers between devices, shards(): lifted = add_rows(lax.all_gather(fc1_weight, 'req', axis=0, tiled=True))  138 us
    all_gather x1, waiting for transfers between devices, shards(): projected = add_rows(lax.all_gather(qkv_local, 'req', axis=0, tiled=True))  135 us
    all_gather x1, waiting for transfers between devices, shards(): lax.all_gather(dense_weight, 'req', axis=1, tiled=True)  100 us
    pmin x1, blocking collectives, shards(): starts = lax.pmin(earliest_rows, 'req')  34.2 us
    all_to_all x1, waiting for transfers between devices, shards(): lax.all_to_all(outgoing.reshape(req_count, page_cap, PAGE * 2 * head_cols...  22.2 us
  transfers between devices with their start and end apart: 10, of which 8 were waited for; matrix products, arithmetic and copies ran while one was open for 6% of the time, Pallas kernels for 0%

commit v1 on v0

--- a/solution.py
+++ b/solution.py
@@ -205,7 +205,9 @@
     hidden = jax.nn.gelu(lifted + fc1_bias, approximate=True).astype(jnp.bfloat16)
     attn_part = jnp.dot(
         attended,
-        lax.all_gather(dense_weight, "req", axis=1, tiled=True),
+        jnp.concatenate(
+            lax.all_to_all(jnp.stack([dense_weight] * lax.axis_size("req")), "req", 0, 0), axis=1
+        ),
         preferred_element_type=jnp.float32,
     )
     mlp_part = jnp.dot(

time: 681 us -> 545 us (0.80)
  waiting for transfers between devices: 559 us -> 372 us
  blocking collectives: 34.2 us -> 61.2 us
  starting transfers between devices: 21.1 us -> 40.1 us
    all_gather x1 -> x0, waiting for transfers between devices: 100 us -> none  [shards(): lax.all_gather(dense_weight, 'req', axis=1, tiled=True)]
    all_gather x1, waiting for transfers between devices: 140 us -> 94.4 us  [shards(): lax.all_gather(fc2_weight, 'req', axis=1, tiled=True)]
    all_gather x1, waiting for transfers between devices: 135 us -> 92 us  [shards(): projected = add_rows(lax.all_gather(qkv_local, 'req', axis=0, tiled=True))]
    pmin x1, blocking collectives: 34.2 us -> 61.2 us  [shards(): starts = lax.pmin(earliest_rows, 'req')]
    all_to_all x0 -> x1, starting transfers between devices: none -> 18.9 us  [shards(): lax.all_to_all(jnp.stack([dense_weight] * lax.axis_size('req')), 'req', 0...]
  transfers between devices with their start and end apart: 10 -> 10, of which waited for: 8 -> 7; matrix products, arithmetic and copies ran while one was open for 6% -> 8% of each run, Pallas kernels for 0% -> 0%
where the time goes in v1:
time: 545 us; the launch traced here: 544 us
  waiting for transfers between devices  372 us (68%)
  blocking collectives  61.2 us (11%)
  starting transfers between devices  40.1 us (7%)
  matrix products  23.1 us (4%)
  other arithmetic  18.1 us (3%)
  between operations  14.4 us (3%)
  local copies, waits for them, and re-layouts  13.2 us (2%)
    all_gather x1, waiting for transfers between devices, shards(): lifted = add_rows(lax.all_gather(fc1_weight, 'req', axis=0, tiled=True))  140 us
    all_gather x1, waiting for transfers between devices, shards(): lax.all_gather(fc2_weight, 'req', axis=1, tiled=True)  94.4 us
    all_gather x1, waiting for transfers between devices, shards(): projected = add_rows(lax.all_gather(qkv_local, 'req', axis=0, tiled=True))  92 us
    pmin x1, blocking collectives, shards(): starts = lax.pmin(earliest_rows, 'req')  61.2 us
    all_to_all x1, waiting for transfers between devices, shards(): lax.all_to_all(outgoing.reshape(req_count, page_cap, PAGE * 2 * head_cols...  22.2 us
    all_to_all x1, starting transfers between devices, shards(): lax.all_to_all(jnp.stack([dense_weight] * lax.axis_size('req')), 'req', 0...  18.9 us
    all_to_all x1, waiting for transfers between devices, shards(): lax.all_to_all(filled.reshape(req_count, page_cap), 'req', split_axis=0,...  12.6 us
  transfers between devices with their start and end apart: 10, of which 7 were waited for; matrix products, arithmetic and copies ran while one was open for 8% of the time, Pallas kernels for 0%

profile of v1, /device:TPU:2, one launch (start us, length us, event | category | flops | bytes accessed | tf_op | source)
XLA Modules:
  0.0 544.5 jit_solution(3886715307231017203)
XLA Ops:
  7.3 0.7 all-gather.5.cloned.1.call-update
  8.0 1.4 copy.52
  9.5 0.7 all-gather.11.cloned.1.call-update
  10.2 1.8 stack.5
  12.0 18.9 %all-to-all-start = ((bf16[64,256,32]{1,2,0:T(8,128)(2,1)}), bf16[64,256,32]{1,2,0:T(8,128)(2,1)S(1)}, u32[]{:S(2)}, u32[]{:S(2)}) async-start(bf16[64,256,32]{1,2,0:T(8,128)(2,1)} %stack.5), calls=%async_computation | async-start | bytes 2097152 | tf_op jit(solution)/shard_map/all_to_all | solution.py:209
  30.9 0.5 all-gather.9.cloned.1.call-update
  31.7 61.2 %pmin.7 = s32[43]{0:T(128)S(1)} all-reduce(s32[43]{0:T(128)S(1)} %select_reduce_fusion.6), channel_id=1, replica_groups=mesh['req'=64,'tensor'=8] {'req'}, use_global_device_ids=true, to_apply=%region_3.4 | all-reduce | flops 43 | bytes 344 | tf_op jit(solution)/shard_map/pmin | solution.py:127
  92.9 0.7 fusion.57
  93.6 0.8 select_reduce_fusion.9
  94.4 0.7 reduce_or.36
  95.3 1.9 constant_dynamic-update-slice_fusion.8
  97.3 1.9 constant_dynamic-update-slice_fusion.4
  99.5 0.2 copy.43
  99.7 0.1 multiply_cosine_fusion
  99.9 1.5 convert_reduce_fusion
  101.4 1.6 fusion.23
  103.1 92.0 %all-gather.7.cloned.1.call-done = bf16[2048,768]{1,0:T(8,128)(2,1)} async-done(((bf16[32,768]{1,0:T(8,128)(2,1)}), bf16[2048,768]{1,0:T(8,128)(2,1)}) %all-gather.7.cloned.1.call-update) | async-done | bytes 3145744 | tf_op jit(solution)/shard_map/all_gather | solution.py:133
  195.1 4.0 convolution_add_fusion.1
  199.1 1.4 copy.41
  200.7 1.9 collective-permute-start
  202.6 4.1 collective-permute-start.1
  206.7 1.9 constant_dynamic-update-slice_fusion
  208.7 3.0 collective-permute-done
  211.7 5.8 %collective-permute-done.1 = bf16[512,2,256]{0,2,1:T(8,128)(2,1)S(1)} collective-permute-done((bf16[512,2,256]{0,2,1:T(8,128)(2,1)S(1)}, bf16[512,2,256]{0,2,1:T(8,128)(2,1)S(1)}, u32[]{:S(2)}, u32[]{:S(2)}) %collective-permute-start.1) | collective-permute-done | bytes 524320 | tf_op jit(solution)/shard_map/ppermute | solution.py:18
  217.6 1.0 slice_bitcast_fusion
  218.6 19.6 %while.11 = (s32[]{:T(128)}, bf16[4,256,64]{1,2,0:T(8,128)(2,1)S(1)}, s32[4]{0:T(128)S(1)}, bf16[256,256]{0,1:T(8,128)(2,1)S(1)}, bf16[1536,256]{0,1:T(8,128)(2,...) while((s32[]{:T(128)}, ...), condition=%wide.region_25.26_spmd.clone, body=%wide.region_22.25_spmd.clone.sunk | while | flops 112492032 | bytes 5240527 | solution.py:88
  218.6 0.6 dynamic_slice.34
  219.8 1.8 fusion.74
  221.6 0.9 fusion.75
  222.5 0.9 fusion.76
  223.5 0.6 dynamic_slice.34
  224.7 1.8 fusion.74
  226.5 0.9 fusion.75
  227.4 0.9 fusion.76
  228.4 0.6 dynamic_slice.34
  229.6 1.8 fusion.74
  231.4 0.9 fusion.75
  232.3 0.9 fusion.76
  233.2 0.6 dynamic_slice.34
  234.5 1.8 fusion.74
  236.3 0.9 fusion.75
  237.2 0.9 fusion.76
  238.2 1.8 fusion.59
  240.0 94.4 %all-gather.11.cloned.1.call-done = bf16[512,2048]{0,1:T(8,128)(2,1)} async-done(((bf16[512,32]{0,1:T(8,128)(2,1)}), bf16[512,2048]{0,1:T(8,128)(2,1)}) %all-gather.11.cloned.1.call-update) | async-done | bytes 2097168 | tf_op jit(solution)/shard_map/all_gather | solution.py:215
  334.5 139.8 %all-gather.9.cloned.1.call-done = bf16[2048,512]{1,0:T(8,128)(2,1)} async-done(((bf16[32,512]{1,0:T(8,128)(2,1)}), bf16[2048,512]{1,0:T(8,128)(2,1)}) %all-gather.9.cloned.1.call-update) | async-done | bytes 2097168 | tf_op jit(solution)/shard_map/all_gather | solution.py:134
  474.3 5.7 %convolution_add_fusion = f32[256,2048]{1,0:T(8,128)} fusion(f32[256,2048]{1,0:T(8,128)} %fusion.59, bf16[512,2048]{0,1:T(8,128)(2,1)} %all-gather.11.cloned.1.call-done, bf16[2048,512]{1,0:T(8,128)(2,1)} %all-gather.9.cloned.1.call-done, f32[512]{0:T(512)S(1)} %copy-done.23, bf16[256,2048]{1,0:T(8,128)(2,1)S(1)} %copy-done, f32[2048]{0:T(1024)S(1)} %copy-done.20, ...), kind=kOutput, calls=%fused_computation.21 | convolution fusion | flops 1078722560 | bytes 9457664 | tf_op jit(solution)/shard_map/dot_general | solution.py:213
  480.0 0.6 copy-done.11
  480.8 0.2 select_reduce_fusion.7
  481.1 0.8 all_to_all.16
  481.9 10.3 %all-to-all-start.1 = ((bf16[64,1,2]{2,1,0:T(2,128)(2,1)}), bf16[64,1,2]{2,1,0:T(2,128)(2,1)S(1)}, u32[]{:S(2)}, u32[]{:S(2)}) async-start(bf16[64,1,2]{2,1,0:T(2,128)(2,1)} %all_to_all.16), calls=%async_computation.2 | async-start | bytes 65536 | tf_op jit(solution)/shard_map/all_to_all | solution.py:167
  492.2 0.2 copy.48
  492.4 0.2 reshape.263
  492.6 0.4 convolution_convert_fusion.1
  493.0 1.1 reshape.264
  494.2 12.6 %all-to-all-done.1 = bf16[64,1,2]{2,1,0:T(2,128)(2,1)S(1)} async-done(((bf16[64,1,2]{2,1,0:T(2,128)(2,1)}), bf16[64,1,2]{2,1,0:T(2,128)(2,1)S(1)}, u32[]{:S(2)}, u32[]{:S(2)}) %all-to-all-start.1) | async-done | bytes 288 | tf_op jit(solution)/shard_map/all_to_all | solution.py:167
  506.8 4.8 all-to-all-start.2
  511.6 0.4 reshape.266
  512.1 0.1 compare_reduce_fusion
  512.2 0.1 gt.16
  512.5 22.2 %all-to-all-done.2 = bf16[64,2,2048]{2,1,0:T(2,128)(2,1)S(1)} async-done(((bf16[64,2,2048]{2,1,0:T(2,128)(2,1)}), bf16[64,2,2048]{2,1,0:T(2,128)(2,1)S(1)}, u32[]{:S(2)}, u32[]{:S(2)}) %all-to-all-start.2) | async-done | bytes 524320 | tf_op jit(solution)/shard_map/all_to_all | solution.py:160
  534.6 0.2 reshape.265
  534.8 0.3 fusion.22
  535.1 1.2 reshape.267
  536.3 1.6 add_convert_fusion
  (97 shorter events, 1.6 us)
Async XLA Ops:
  7.2 24.4 %copy-start.15 = (s32[256]{0:T(256)S(1)}, s32[256]{0:T(256)}, u32[]{:S(2)}) copy-start(s32[256]{0:T(256)} %param.20) | copy-start | bytes 3076
  7.2 86.5 %copy-start.12 = (s32[43]{0:T(128)S(1)}, s32[43]{0:T(128)}, u32[]{:S(2)}) copy-start(s32[43]{0:T(128)} %param.21) | copy-start | bytes 520
  7.2 92.3 %copy-start.8 = (f32[3,256]{1,0:T(4,128)S(1)}, f32[3,256]{1,0:T(4,128)}, u32[]{:S(2)}) copy-start(f32[3,256]{1,0:T(4,128)} %param.27) | copy-start | bytes 9220
  7.2 92.3 %copy-start.3 = (bf16[256,2,256]{2,1,0:T(2,128)(2,1)S(1)}, bf16[256,2,256]{2,1,0:T(2,128)(2,1)}, u32[]{:S(2)}) copy-start(bf16[256,2,256]{2,1,0:T(2,128)(2,1)} %param.34) | copy-start | bytes 786436
  7.2 92.7 %all-gather.5.cloned.1.call-start = ((), (), s32[]{:S(2)}) async-start(), calls=%async_computation.4 | async-start | bytes 1179648 | tf_op jit(solution)/shard_map/all_gather | solution.py:118
  7.9 187.1 %all-gather.7.cloned.1.call-start = ((), (), s32[]{:S(2)}) async-start(), calls=%async_computation.5 | async-start | bytes 3194880 | tf_op jit(solution)/shard_map/all_gather | solution.py:133
  9.4 325.0 %all-gather.11.cloned.1.call-start = ((), (), s32[]{:S(2)}) async-start(), calls=%async_computation.7 | async-start | bytes 2129920 | tf_op jit(solution)/shard_map/all_gather | solution.py:215
  12.0 183.1 %copy-start.19 = (f32[2048]{0:T(1024)S(1)}, f32[2048]{0:T(1024)}, u32[]{:S(2)}) copy-start(f32[2048]{0:T(1024)} %param.25) | copy-start | bytes 24580
  12.0 183.1 %copy-start.21 = (f32[2048]{0:T(1024)S(1)}, f32[2048]{0:T(1024)}, u32[]{:S(2)}) copy-start(f32[2048]{0:T(1024)} %param.24) | copy-start | bytes 24580
  12.0 226.2 %all-to-all-start = ((bf16[64,256,32]{1,2,0:T(8,128)(2,1)}), bf16[64,256,32]{1,2,0:T(8,128)(2,1)S(1)}, u32[]{:S(2)}, u32[]{:S(2)}) async-start(bf16[64,256,32]{1,2,0:T(8,128)(2,1)} %stack.5), calls=%async_computation | async-start | bytes 2097152 | tf_op jit(solution)/shard_map/all_to_all | solution.py:209
  30.9 443.4 %all-gather.9.cloned.1.call-start = ((), (), s32[]{:S(2)}) async-start(), calls=%async_computation.6 | async-start | bytes 2129920 | tf_op jit(solution)/shard_map/all_gather | solution.py:134
  31.4 504.9 %reduce-scatter.2.cloned.1.call-start = ((), (), s32[]{:S(2)}) async-start(), calls=%async_computation.8 | async-start | bytes 2359296 | tf_op jit(solution)/shard_map/reduce_scatter | solution.py:219
  95.3 99.8 %copy-start.4 = (s32[256]{0:T(256)}, s32[256]{0:T(256)S(1)}, u32[]{:S(2)}) copy-start(s32[256]{0:T(256)S(1)} %get-tuple-element.253) | copy-start | bytes 3076
  99.4 95.7 %copy-start.6 = (s32[256]{0:T(256)}, s32[256]{0:T(256)S(1)}, u32[]{:S(2)}) copy-start(s32[256]{0:T(256)S(1)} %get-tuple-element.256) | copy-start | bytes 3076
  99.9 95.2 %copy-start = (bf16[256,2048]{1,0:T(8,128)(2,1)S(1)}, bf16[256,2048]{1,0:T(8,128)(2,1)}, u32[]{:S(2)}) copy-start(bf16[256,2048]{1,0:T(8,128)(2,1)} %all-gather.5.cloned.1.call-done) | copy-start | bytes 3145732
  101.4 97.6 %copy-start.9 = (f32[256]{0:T(256)}, f32[256]{0:T(256)S(1)}, u32[]{:S(2)}) copy-start(f32[256]{0:T(256)S(1)} %broadcast_multiply_fusion) | copy-start | bytes 3076
  103.1 96.0 %copy-start.16 = (f32[256]{0:T(256)}, f32[256]{0:T(256)S(1)}, u32[]{:S(2)}) copy-start(f32[256]{0:T(256)S(1)} %add_rsqrt_fusion) | copy-start | bytes 3076
  200.7 11.0 %collective-permute-start = (bf16[512,2,256]{0,2,1:T(8,128)(2,1)S(1)}, bf16[512,2,256]{0,2,1:T(8,128)(2,1)S(1)}, u32[]{:S(2)}, u32[]{:S(2)}) collective-permute-start(bf16[512,2,256]{0,2,1:T(8,128)(2,1)S(1)} %pad_maximum_fusion.1), channel_id=1, source_target_pairs={{0,8},{8,16},{16,24},{24,32},{32,40},{40,48},{48,56},{56,64},{64,7... | collective-permute-start | bytes 1572872 | tf_op jit(solution)/shard_map/ppermute | solution.py:18
  202.6 14.9 %collective-permute-start.1 = (bf16[512,2,256]{0,2,1:T(8,128)(2,1)S(1)}, bf16[512,2,256]{0,2,1:T(8,128)(2,1)S(1)}, u32[]{:S(2)}, u32[]{:S(2)}) collective-permute-start(bf16[512,2,256]{0,2,1:T(8,128)(2,1)S(1)} %pad_maximum_fusion.1), channel_id=1, source_target_pairs={{0,16},{8,24},{16,32},{24,40},{32,48},{40,56},{48,64},{56,72},{64,... | collective-permute-start | bytes 1572872 | tf_op jit(solution)/shard_map/ppermute | solution.py:18
  217.6 1.0 copy-start.5
  217.6 1.0 copy-start.7
  238.1 236.1 %copy-start.10 = (f32[256]{0:T(256)S(1)}, f32[256]{0:T(256)}, u32[]{:S(2)}) copy-start(f32[256]{0:T(256)} %copy-done.9) | copy-start | bytes 3076
  238.1 236.1 %copy-start.17 = (f32[256]{0:T(256)S(1)}, f32[256]{0:T(256)}, u32[]{:S(2)}) copy-start(f32[256]{0:T(256)} %copy-done.16) | copy-start | bytes 3076
  238.2 236.1 %copy-start.20 = (f32[2048]{0:T(1024)S(1)}, f32[2048]{0:T(1024)}, u32[]{:S(2)}) copy-start(f32[2048]{0:T(1024)} %param.25) | copy-start | bytes 24580
  238.2 236.1 %copy-start.22 = (f32[2048]{0:T(1024)S(1)}, f32[2048]{0:T(1024)}, u32[]{:S(2)}) copy-start(f32[2048]{0:T(1024)} %param.24) | copy-start | bytes 24580
  238.2 236.1 %copy-start.23 = (f32[512]{0:T(512)S(1)}, f32[512]{0:T(512)}, u32[]{:S(2)}) copy-start(f32[512]{0:T(512)} %param.31) | copy-start | bytes 6148
  480.0 0.7 copy-start.11
  481.9 24.9 %all-to-all-start.1 = ((bf16[64,1,2]{2,1,0:T(2,128)(2,1)}), bf16[64,1,2]{2,1,0:T(2,128)(2,1)S(1)}, u32[]{:S(2)}, u32[]{:S(2)}) async-start(bf16[64,1,2]{2,1,0:T(2,128)(2,1)} %all_to_all.16), calls=%async_computation.2 | async-start | bytes 65536 | tf_op jit(solution)/shard_map/all_to_all | solution.py:167
  492.2 19.4 %copy-start.1 = (bf16[512,2,256]{2,1,0:T(2,128)(2,1)S(1)}, bf16[512,2,256]{2,1,0:T(2,128)(2,1)}, u32[]{:S(2)}) copy-start(bf16[512,2,256]{2,1,0:T(2,128)(2,1)} %param.35) | copy-start | bytes 1572868
  492.6 19.7 %copy-start.18 = (s32[1,128]{1,0:T(1,128)S(1)}, s32[1,128]{1,0:T(1,128)}, u32[]{:S(2)}) copy-start(s32[1,128]{1,0:T(1,128)} %param.23) | copy-start | bytes 1540
  506.8 27.8 %all-to-all-start.2 = ((bf16[64,2,2048]{2,1,0:T(2,128)(2,1)}), bf16[64,2,2048]{2,1,0:T(2,128)(2,1)S(1)}, u32[]{:S(2)}, u32[]{:S(2)}) async-start(bf16[64,2,2048]{2,1,0:T(2,128)(2,1)} %reshape.264), calls=%async_computation.3 | async-start | bytes 1048576 | tf_op jit(solution)/shard_map/all_to_all | solution.py:160
  512.0 24.3 %copy-start.2 = (bf16[256,256]{1,0:T(8,128)(2,1)S(1)}, bf16[256,256]{1,0:T(8,128)(2,1)}, u32[]{:S(2)}) copy-start(bf16[256,256]{1,0:T(8,128)(2,1)} %param.19) | copy-start | bytes 393220
  512.0 24.3 %copy-start.13 = (f32[256]{0:T(256)S(1)}, f32[256]{0:T(256)}, u32[]{:S(2)}) copy-start(f32[256]{0:T(256)} %param.33) | copy-start | bytes 3076
  512.1 24.3 %copy-start.14 = (f32[256]{0:T(256)S(1)}, f32[256]{0:T(256)}, u32[]{:S(2)}) copy-start(f32[256]{0:T(256)} %param.29) | copy-start | bytes 3076
Sparse Core Ops, SparseCore 0:
  10.2 34.8 all-gather.4
  48.6 146.4 all-gather.6
  198.0 136.3 all-gather.10
  337.3 136.9 all-gather.8
  480.1 34.3 reduce-scatter.1
